TPU v7x, 32 devices: a whole 2x2x4 slice. The times are simulated.
32 devices in a mesh: grp: 2 (over x), col: 16 (over z, y, core).
Axes of the slice: x: 2, y: 2, z: 4, core: 2. Of those that a mesh axis runs over, the one named last changes fastest.
Arguments:
- database: int32 [256, 4096], P('col', 'grp'), parts along dimension 1, may hold values from 0 to 255
- queries: int32 [16, 256], P('grp', 'col'), parts along dimension 0, may hold values from -2147483648 to 2147483646
- key_rows: int32 [16, 8192], P('grp', 'col'), parts along dimension 0, may hold values from -2147483648 to 2147483646
- hint: int32 [4, 1024], P('grp'), parts along dimension 0, may hold values from -2147483648 to 2147483646
- assignment: int32 [32], P('grp'), parts along dimension 0, may hold values from 0 to 15, each once
Outputs:
- packed: float32 [32, 2, 1024], P(('grp', 'col')), parts along dimension 0
There are 2 independent parts, one for each index of `grp`. A program takes and returns all parts, laid end to end along the dimension named above; each array names one. Nothing has to cross between parts.
Inputs may be any that keep to these rules, and one draw needn't show every extreme that they name: `assignment`: every unit appears in exactly one slot.
All inputs are finite; a program needn't handle non-finite values.
Results may differ from a plain program's by a relative error of at most 0.0003.
Values sent between devices are 32-bit elements; how exact they have to be, the bound alone decides.
A program may use at most 128 MiB of HBM per device.

v0:
```python
import functools

import jax
import jax.numpy as jnp
from jax import lax
from jax.experimental import pallas as pl
from jax.experimental.pallas import tpu as pltpu
from jax.sharding import PartitionSpec as P

LEVELS = 2
DIGITS = 2
LANES = 128
WORD_BYTES = 4
DIGIT_BYTES = WORD_BYTES // DIGITS
SPAN = LANES // DIGIT_BYTES


def iota(shape, axis):
    return lax.broadcasted_iota(jnp.int32, shape, axis)


def byte_of(words, index):
    return jnp.bitwise_and(jnp.right_shift(words, 8 * index), 255).astype(jnp.float32)


def shifted(poly, amount):
    rows = poly.shape[0]
    amount = amount % (2 * rows * LANES)
    negate, turn = divmod(amount // LANES, rows)
    moved = poly
    if turn:
        moved = pltpu.roll(poly, turn, 0)
        moved = jnp.where(iota(poly.shape, 0) >= turn, moved, -moved)
    return -moved if negate else moved


def automorph(poly, level):
    step = poly.shape[0] * LANES >> level
    period = 2 << level
    residue = jnp.bitwise_and(iota(poly.shape, 1), period - 1)
    out = poly
    for m in range(1, period):
        out = jnp.where(residue == m, shifted(poly, step * m), out)
    return out


def fill_toeplitz(word_poly, toeplitz):
    rows = word_poly.shape[0]
    block = (SPAN, LANES)
    ahead = iota(block, 1) >= iota(block, 0)

    def turned(q):
        row = jnp.broadcast_to(word_poly[q : q + 1], block)
        return pltpu.roll(row, 0, 1, stride=1, stride_axis=0)

    before = turned(rows - 1)
    for q in range(rows):
        here = turned(q)
        words = jnp.where(ahead, here, before)
        for b in range(WORD_BYTES):
            part = byte_of(words, b)
            if q == 0:
                part = jnp.where(ahead, part, -part)
            toeplitz[b * SPAN : (b + 1) * SPAN, q * LANES : (q + 1) * LANES] = part.astype(
                jnp.bfloat16
            )
        before = here


def spread(tile):
    first = iota(tile.shape, 1) < SPAN
    turned = pltpu.roll(tile, SPAN, 1)
    return [
        jnp.where(first, tile, jnp.left_shift(turned, 8)),
        jnp.where(first, turned, jnp.left_shift(tile, 8)),
    ]


def key_side(keys):
    blocks = []
    for s in range(WORD_BYTES):
        for p in range(len(keys[0])):
            for h in range(DIGIT_BYTES):
                tiles = [byte_of(digit_keys[p][h], s) for digit_keys in keys]
                blocks.append(jnp.concatenate(tiles, axis=1))
    return jnp.concatenate(blocks, axis=0).astype(jnp.bfloat16)


def switch(toeplitz, key_polys, rows):
    sides = len(key_polys[0])
    products = jnp.dot(
        key_side(key_polys), toeplitz, preferred_element_type=jnp.float32
    ).astype(jnp.int32)
    lane = iota((rows, LANES), 1)
    sums = []
    for p in range(sides):
        total = jnp.zeros((rows, LANES), jnp.int32)
        for h in range(DIGIT_BYTES):
            words = None
            for s in range(WORD_BYTES):
                at = ((s * sides + p) * DIGIT_BYTES + h) * rows
                term = jnp.left_shift(products[at : at + rows], 8 * s)
                words = term if words is None else words + term
            out = words[:, :LANES]
            for q in range(1, rows):
                out = out + shifted(words[:, q * LANES : (q + 1) * LANES], q * LANES)
            if h:
                turn = h * SPAN
                carried = pltpu.roll(shifted(out, LANES), turn, 1)
                out = jnp.where(lane >= turn, pltpu.roll(out, turn, 1), carried)
            total = total + out
        sums.append(total)
    return sums


def kernel(
    n, slots, share, width, assign_hbm, database_hbm, queries_hbm, keys_hbm, hint_hbm, out,
    assign, database, queries, keys, hint, loaded, unit_part, unit_keys, masks,
    ans_send, key_send, ans_recv, key_recv, key_words, toeplitz,
    ready, ans_got, key_got,
):
    me = lax.axis_index("col")
    clients, columns = queries.shape
    polys, cycle = hint.shape
    rows = cycle // LANES
    key_rows = key_send.shape[1] // slots
    key_pitch = unit_keys.shape[1]
    unit_key_rows = unit_keys.reshape(clients * polys * key_pitch, LANES)
    unit_part_rows = unit_part.reshape(clients * polys * rows, LANES)
    chunks = 4
    chunk = database.shape[1] // chunks
    size = 2
    planes = n // size
    few = n <= LANES // 8
    level_blocks = n // LEVELS
    chip = lax.div(me, size)
    partner = me + 1 - 2 * lax.rem(me, size)
    height = planes // width
    across = lax.rem(chip, width)
    along = lax.div(chip, width)
    poly_blocks = n // (LEVELS * DIGITS * 2)
    kind_held = jnp.where(me >= n - poly_blocks, LEVELS, lax.div(me, level_blocks))

    def each(count, body, start=0):
        lax.fori_loop(start, count, lambda i, c: (body(i), c)[1], 0, unroll=few)
    loads = [
        pltpu.make_async_copy(source, target, loaded.at[min(i, 2)])
        for i, (source, target) in enumerate(
            (
                (assign_hbm, assign),
                (keys_hbm, keys),
                (queries_hbm, queries),
                (database_hbm, database),
                (hint_hbm, hint),
            )
        )
    ]
    for i, load in enumerate(loads):
        if i == 3:
            for j in range(chunks):
                at = pl.ds(j * chunk, chunk)
                pltpu.make_async_copy(database_hbm.at[:, at], database.at[:, at], loaded.at[2]).start()
        else:
            load.start()
    def span(start, stop, body):
        lax.fori_loop(start, stop, lambda i, c: (body(i), c)[1], 0)

    def on_chips(start, stop, column, body):
        def both(i):
            first = (i * width + column) * size
            for core in range(size):
                body(first + core)

        span(start, stop, both)

    sent = loaded.at[0]
    barrier = pltpu.get_barrier_semaphore()

    def greet(there):
        pl.semaphore_signal(barrier, inc=1, device_id={"col": there})

    greet(partner)
    for column in range(width):
        on_chips(
            jnp.where(column < across, height, along + jnp.where(column == across, 1, 0)),
            height,
            column,
            greet,
        )
    pl.semaphore_wait(barrier, (along + 1) * (across + 1) * size - 1)

    def announce(stage, chips):
        @pl.when(chip == chips - 1)
        def _():
            def tell(i):
                there = i * size + lax.rem(me, size)
                pl.semaphore_signal(ready.at[stage], inc=1, device_id={"col": there})

            span(0, chips - 1, tell)

    announce(0, planes // 2)
    announce(1, planes)
    loads[0].wait()
    loads[1].wait()
    lane_owner = iota((clients, LANES), 1) // (LANES // share)
    for j in range(key_rows):
        tile = keys[:, j * LANES : (j + 1) * LANES]
        if share > 1:
            tile = jnp.where(lane_owner == lax.rem(me, share), tile, 0)
        for p in range(polys):
            unit_key_rows[pl.ds(p * key_pitch + j, clients, stride=polys * key_pitch), :] = tile

    def stage_keys(owner):
        for k in range(slots):
            key_send[owner, k * key_rows : (k + 1) * key_rows, :] = unit_keys[assign[owner * slots + k]][:key_rows]

    def stage_answers(owner):
        for k in range(slots):
            ans_send[owner, k * rows : (k + 1) * rows, :] = unit_part[assign[owner * slots + k]]
    each(n, stage_keys)

    def send_keys(there):
        pltpu.make_async_remote_copy(
            src_ref=key_send.at[there],
            dst_ref=key_recv.at[me],
            send_sem=sent,
            recv_sem=key_got.at[kind_held],
            device_id={"col": there},
        ).start()

    def send_answers(there):
        pltpu.make_async_remote_copy(
            src_ref=ans_send.at[there],
            dst_ref=ans_recv.at[me],
            send_sem=sent,
            recv_sem=ans_got,
            device_id={"col": there},
        ).start()

    def to_first(send):
        @pl.when(chip > 0)
        def _():
            for core in range(size):
                send(core)

    def to_early(send):
        for column in range(width):
            on_chips(
                0 if column else 1,
                jnp.where(column > across, 0, along + jnp.where(column == across, 0, 1)),
                column,
                send,
            )
        send(partner)

    def to_late(stage, send):
        for column in range(width):
            start = jnp.where(column > across, 0, along + 1)
            if stage:
                start = jnp.maximum(start, jnp.where(along < height // 2, height // 2, 0))
            on_chips(start, height // 2 if stage == 0 else height, column, send)
    to_first(send_keys)
    pltpu.make_async_copy(key_send.at[me], key_recv.at[me], key_got.at[kind_held]).start()
    for load in loads[2:]:
        load.wait()
    query_words = queries[...]
    query_bytes = jnp.concatenate(
        [byte_of(query_words, b) for b in range(WORD_BYTES)], axis=0
    ).astype(jnp.bfloat16)
    products = jnp.dot(
        query_bytes,
        database[...].astype(jnp.float32).astype(jnp.bfloat16),
        preferred_element_type=jnp.float32,
    ).astype(jnp.int32)
    partial = products[:clients]
    for b in range(1, WORD_BYTES):
        partial = partial + jnp.left_shift(products[b * clients : (b + 1) * clients], 8 * b)
    for j in range(polys * rows):
        unit_part_rows[pl.ds(j, clients, stride=polys * rows), :] = partial[:, j * LANES : (j + 1) * LANES]
    each(n, stage_answers)
    to_first(send_answers)
    to_early(send_keys)
    to_early(send_answers)
    pltpu.make_async_copy(ans_send.at[me], ans_recv.at[me], ans_got).start()
    for p in range(polys):
        for q in range(rows):
            masks[p, q : q + 1, :] = hint[p : p + 1, q * LANES : (q + 1) * LANES]

    def first_mask(k):
        return masks[lax.rem(assign[me * slots + k], polys)]

    fill_toeplitz(automorph(first_mask(0), 0), toeplitz)
    def when_ready(stage, chips):
        @pl.when((along < chips // width) & (chip != chips - 1))
        def _():
            pl.semaphore_wait(ready.at[stage], 1)
            to_late(stage, send_keys)
            to_late(stage, send_answers)

    when_ready(0, planes // 2)

    when_ready(1, planes)

    def wait_blocks(buffer, semaphore, start, count):
        blocks = buffer.at[pl.ds(start, count)]
        pltpu.make_async_copy(blocks, blocks, semaphore).wait()
    switched = []

    def gather_keys(k, kind, start, stop):
        if k == 0:
            wait_blocks(key_recv, key_got.at[kind], start, stop - start)
        for j in range(start // share, stop // share):
            block = key_recv[j * share, k * key_rows : (k + 1) * key_rows, :]
            for i in range(1, share):
                block = block + key_recv[j * share + i, k * key_rows : (k + 1) * key_rows, :]
            key_words[j * key_rows : (j + 1) * key_rows, :] = block

    def key_poly(level, t, p):
        at = ((level * DIGITS + t) * 2 + p) * rows
        return spread(key_words[at : at + rows, :])

    for k in range(slots):
        mask = first_mask(k)
        if k:
            fill_toeplitz(automorph(mask, 0), toeplitz)
        added = []
        for level in range(LEVELS):
            if level:
                fill_toeplitz(automorph(mask, level), toeplitz)
            last = level == LEVELS - 1
            stop = (level + 1) * level_blocks
            gather_keys(k, level, level * level_blocks, stop - (poly_blocks if last else 0))
            polys_held = [[key_poly(level, t, p) for p in range(2)] for t in range(DIGITS)]
            if last:
                zero = jnp.zeros((rows, LANES), jnp.int32)
                polys_held[-1][-1] = [zero] * DIGIT_BYTES
            to_mask, to_value = switch(toeplitz[...], polys_held, rows)
            mask = mask + to_mask
            if last:
                gather_keys(k, LEVELS, stop - poly_blocks, stop)
                tail = switch(toeplitz[-DIGIT_BYTES * SPAN :, :], [[key_poly(level, DIGITS - 1, 1)]], rows)
                to_value = to_value + tail[0]
            added.append(to_value)
        switched.append((mask, added))
    wait_blocks(ans_recv, ans_got, 0, n)
    for k, (mask, added) in enumerate(switched):
        value = ans_recv[0, k * rows : (k + 1) * rows, :]
        for j in range(1, n):
            value = value + ans_recv[j, k * rows : (k + 1) * rows, :]
        for level in range(LEVELS):
            value = value + automorph(value, level) + added[level]
        for index, words in enumerate((mask, value)):
            scaled = words.astype(jnp.float32) * 2.0 ** (-32)
            for q in range(rows):
                out[k, index : index + 1, q * LANES : (q + 1) * LANES] = scaled[q : q + 1]
    wait_blocks(key_send, sent, 0, n - 1)
    wait_blocks(ans_send, sent, 0, n - 1)


def solution(mesh):
    n = mesh.shape["col"]
    across = 2

    def on_device(database, queries, key_rows, hint, assignment):
        clients = queries.shape[0]
        polys, cycle = hint.shape
        rows = cycle // LANES
        slots = assignment.shape[0] // n
        width = key_rows.shape[1]
        share = max(1, LANES // width)
        if share > 1:
            key_rows = jnp.tile(key_rows, (1, share))
        tiles = key_rows.shape[1] // LANES
        place = pl.BlockSpec(memory_space=pltpu.HBM)
        return pl.pallas_call(
            functools.partial(kernel, n, slots, share, across),
            out_shape=pltpu.VMEM((slots, 2, cycle), jnp.float32),
            in_specs=[place] * 5,
            out_specs=pl.BlockSpec(memory_space=pltpu.VMEM),
            scratch_shapes=[
                pltpu.SMEM(assignment.shape, jnp.int32),
                pltpu.VMEM(database.shape, jnp.int32),
                pltpu.VMEM(queries.shape, jnp.int32),
                pltpu.VMEM(key_rows.shape, jnp.int32),
                pltpu.VMEM(hint.shape, jnp.int32),
                pltpu.SemaphoreType.DMA((3,)),
                pltpu.VMEM((polys * clients, rows, LANES), jnp.int32),
                pltpu.VMEM((polys * clients, -(-tiles // 8) * 8, LANES), jnp.int32),
                pltpu.VMEM((polys, rows, LANES), jnp.int32),
                pltpu.VMEM((n, slots * rows, LANES), jnp.int32),
                pltpu.VMEM((n, slots * tiles, LANES), jnp.int32),
                pltpu.VMEM((n, slots * rows, LANES), jnp.int32),
                pltpu.VMEM((n, slots * tiles, LANES), jnp.int32),
                pltpu.VMEM((n // share * tiles, LANES), jnp.int32),
                pltpu.VMEM((WORD_BYTES * SPAN, cycle), jnp.bfloat16),
                pltpu.SemaphoreType.REGULAR((2,)),
                pltpu.SemaphoreType.DMA,
                pltpu.SemaphoreType.DMA((LEVELS + 1,)),
            ],
            compiler_params=pltpu.CompilerParams(
                collective_id=0, has_side_effects=True
            ),
        )(*(pltpu.with_memory_space_constraint(x, pltpu.HBM) for x in (assignment, database, queries, key_rows, hint)))

    placed = (P("col", "grp"), P("grp", "col"), P("grp", "col"), P("grp", None), P("grp"))
    return jax.shard_map(
        on_device,
        mesh=mesh,
        in_specs=placed,
        out_specs=P(("grp", "col"), None, None),
        check_vma=False,
    )
```

profile of v0, /device:TPU:0, one launch (start us, length us, event | category | flops | bytes accessed | tf_op | source)
XLA Modules:
  0.0 9.4 jit_solution(16058914570277989171)
XLA Ops:
  0.0 8.8 %shard_map.55 = f32[1,2,1024]{2,1,0:T(2,128)S(1)} custom-call(s32[16]{0:T(128)} %assign_hbm.1, s32[16,2048]{1,0:T(8,128)} %database_hbm.1, s32[8,16]{1,0:T(8,128)} %queries_hbm.1, s32[8,512]{1,0:T(8,128)} %keys_hbm.1, s32[2,1024]{1,0:T(2,128)} %hint_hbm.1), custom_call_target="tpu_custom_call" | custom-call | tf_op jit(solution)/shard_map/pallas_call | solution.py:375
  8.8 0.6 %copy.7 = f32[1,2,1024]{2,1,0:T(2,128)} copy(f32[1,2,1024]{2,1,0:T(2,128)S(1)} %shard_map.55) | data formatting | bytes 16384
where the time goes:
time: 9.58 us; the launch traced here: 9.4 us
  Pallas kernels  8.79 us (92%)
  local copies, waits for them, and re-layouts  0.6 us (6%)
    pallas_call x1, Pallas kernels, on_device(): pl.pallas_call(functools.partial(kernel, n, slots, share, across), out_sh...  8.79 us
    unnamed x1, local copies, waits for them, and re-layouts  0.6 us

commit v1 on v0

--- a/solution.py
+++ b/solution.py
@@ -44,27 +44,39 @@
     return out
 
 
-def fill_toeplitz(word_poly, toeplitz):
+def fill_rows(word_poly, table, offset, placed):
     rows = word_poly.shape[0]
     block = (SPAN, LANES)
-    ahead = iota(block, 1) >= iota(block, 0)
+    ahead = iota(block, 1) >= iota(block, 0) + offset
 
     def turned(q):
         row = jnp.broadcast_to(word_poly[q : q + 1], block)
-        return pltpu.roll(row, 0, 1, stride=1, stride_axis=0)
+        return pltpu.roll(row, offset, 1, stride=1, stride_axis=0)
 
     before = turned(rows - 1)
     for q in range(rows):
         here = turned(q)
         words = jnp.where(ahead, here, before)
-        for b in range(WORD_BYTES):
+        for b, at in placed:
             part = byte_of(words, b)
             if q == 0:
                 part = jnp.where(ahead, part, -part)
-            toeplitz[b * SPAN : (b + 1) * SPAN, q * LANES : (q + 1) * LANES] = part.astype(
-                jnp.bfloat16
-            )
+            table[at : at + SPAN, q * LANES : (q + 1) * LANES] = part.astype(jnp.bfloat16)
         before = here
+
+
+def fill_toeplitz(word_poly, toeplitz):
+    fill_rows(word_poly, toeplitz, 0, [(b, b * SPAN) for b in range(WORD_BYTES)])
+
+
+def fill_tail(word_poly, table):
+    for offset in range(0, LANES, SPAN):
+        fill_rows(
+            word_poly,
+            table,
+            offset,
+            [((DIGITS - 1) * DIGIT_BYTES + a, a * LANES + offset) for a in range(DIGIT_BYTES)],
+        )
 
 
 def spread(tile):
@@ -113,10 +125,30 @@
     return sums
 
 
+def switch_tail(table, words):
+    rows = words.shape[0]
+    moved = [jnp.left_shift(words, 8 * a) for a in range(DIGIT_BYTES)]
+    side = jnp.concatenate(
+        [
+            jnp.concatenate([byte_of(part, s) for part in moved], axis=1)
+            for s in range(WORD_BYTES)
+        ],
+        axis=0,
+    ).astype(jnp.bfloat16)
+    products = jnp.dot(side, table, preferred_element_type=jnp.float32).astype(jnp.int32)
+    total = products[:rows]
+    for s in range(1, WORD_BYTES):
+        total = total + jnp.left_shift(products[s * rows : (s + 1) * rows], 8 * s)
+    out = total[:, :LANES]
+    for q in range(1, rows):
+        out = out + shifted(total[:, q * LANES : (q + 1) * LANES], q * LANES)
+    return out
+
+
 def kernel(
     n, slots, share, width, assign_hbm, database_hbm, queries_hbm, keys_hbm, hint_hbm, out,
     assign, database, queries, keys, hint, loaded, unit_part, unit_keys, masks,
-    ans_send, key_send, ans_recv, key_recv, key_words, toeplitz,
+    ans_send, key_send, ans_recv, key_recv, key_words, toeplitz, tail, held,
     ready, ans_got, key_got,
 ):
     me = lax.axis_index("col")
@@ -144,22 +176,22 @@
     def each(count, body, start=0):
         lax.fori_loop(start, count, lambda i, c: (body(i), c)[1], 0, unroll=few)
     loads = [
-        pltpu.make_async_copy(source, target, loaded.at[min(i, 2)])
+        pltpu.make_async_copy(source, target, loaded.at[min(i // 2, 1)])
         for i, (source, target) in enumerate(
             (
                 (assign_hbm, assign),
                 (keys_hbm, keys),
+                (database_hbm, database),
                 (queries_hbm, queries),
-                (database_hbm, database),
                 (hint_hbm, hint),
             )
         )
     ]
     for i, load in enumerate(loads):
-        if i == 3:
+        if i == 2:
             for j in range(chunks):
                 at = pl.ds(j * chunk, chunk)
-                pltpu.make_async_copy(database_hbm.at[:, at], database.at[:, at], loaded.at[2]).start()
+                pltpu.make_async_copy(database_hbm.at[:, at], database.at[:, at], loaded.at[1]).start()
         else:
             load.start()
     def span(start, stop, body):
@@ -277,8 +309,10 @@
         partial = partial + jnp.left_shift(products[b * clients : (b + 1) * clients], 8 * b)
     for j in range(polys * rows):
         unit_part_rows[pl.ds(j, clients, stride=polys * rows), :] = partial[:, j * LANES : (j + 1) * LANES]
-    each(n, stage_answers)
+    for core in range(size):
+        stage_answers(core)
     to_first(send_answers)
+    each(n, stage_answers, size)
     to_early(send_keys)
     to_early(send_answers)
     pltpu.make_async_copy(ans_send.at[me], ans_recv.at[me], ans_got).start()
@@ -317,33 +351,49 @@
 
     def key_poly(level, t, p):
         at = ((level * DIGITS + t) * 2 + p) * rows
-        return spread(key_words[at : at + rows, :])
-
+        return key_words[at : at + rows, :]
+
+    def key_polys(level):
+        return [[spread(key_poly(level, t, p)) for p in range(2)] for t in range(DIGITS)]
+
+    last = LEVELS - 1
     for k in range(slots):
         mask = first_mask(k)
         if k:
             fill_toeplitz(automorph(mask, 0), toeplitz)
         added = []
-        for level in range(LEVELS):
-            if level:
-                fill_toeplitz(automorph(mask, level), toeplitz)
-            last = level == LEVELS - 1
-            stop = (level + 1) * level_blocks
-            gather_keys(k, level, level * level_blocks, stop - (poly_blocks if last else 0))
-            polys_held = [[key_poly(level, t, p) for p in range(2)] for t in range(DIGITS)]
-            if last:
-                zero = jnp.zeros((rows, LANES), jnp.int32)
-                polys_held[-1][-1] = [zero] * DIGIT_BYTES
+        for level in range(last):
+            gather_keys(k, level, level * level_blocks, (level + 1) * level_blocks)
+            to_mask, to_value = switch(toeplitz[...], key_polys(level), rows)
+            mask = mask + to_mask
+            added.append(to_value)
+            turned = automorph(mask, level + 1)
+            fill_toeplitz(turned, toeplitz)
+        early, late = n - level_blocks, n - poly_blocks
+        @pl.when(chip > 0)
+        def _():
+            gather_keys(k, last, early, late)
+            gather_keys(k, LEVELS, late, n)
+            to_mask, to_value = switch(toeplitz[...], key_polys(last), rows)
+            held[k, 0] = mask + to_mask
+            held[k, 1] = to_value
+
+        @pl.when(chip == 0)
+        def _():
+            gather_keys(k, last, early, late)
+            polys_held = key_polys(last)
+            polys_held[-1][-1] = [jnp.zeros((rows, LANES), jnp.int32)] * DIGIT_BYTES
             to_mask, to_value = switch(toeplitz[...], polys_held, rows)
-            mask = mask + to_mask
-            if last:
-                gather_keys(k, LEVELS, stop - poly_blocks, stop)
-                tail = switch(toeplitz[-DIGIT_BYTES * SPAN :, :], [[key_poly(level, DIGITS - 1, 1)]], rows)
-                to_value = to_value + tail[0]
-            added.append(to_value)
-        switched.append((mask, added))
+            held[k, 0] = mask + to_mask
+            fill_tail(turned, tail)
+            gather_keys(k, LEVELS, late, n)
+            held[k, 1] = to_value + switch_tail(tail[...], key_poly(last, DIGITS - 1, 1))
+
+        switched.append(added)
     wait_blocks(ans_recv, ans_got, 0, n)
-    for k, (mask, added) in enumerate(switched):
+    for k, added in enumerate(switched):
+        mask = held[k, 0]
+        added = added + [held[k, 1]]
         value = ans_recv[0, k * rows : (k + 1) * rows, :]
         for j in range(1, n):
             value = value + ans_recv[j, k * rows : (k + 1) * rows, :]
@@ -383,7 +433,7 @@
                 pltpu.VMEM(queries.shape, jnp.int32),
                 pltpu.VMEM(key_rows.shape, jnp.int32),
                 pltpu.VMEM(hint.shape, jnp.int32),
-                pltpu.SemaphoreType.DMA((3,)),
+                pltpu.SemaphoreType.DMA((2,)),
                 pltpu.VMEM((polys * clients, rows, LANES), jnp.int32),
                 pltpu.VMEM((polys * clients, -(-tiles // 8) * 8, LANES), jnp.int32),
                 pltpu.VMEM((polys, rows, LANES), jnp.int32),
@@ -393,6 +443,8 @@
                 pltpu.VMEM((n, slots * tiles, LANES), jnp.int32),
                 pltpu.VMEM((n // share * tiles, LANES), jnp.int32),
                 pltpu.VMEM((WORD_BYTES * SPAN, cycle), jnp.bfloat16),
+                pltpu.VMEM((DIGIT_BYTES * LANES, cycle), jnp.bfloat16),
+                pltpu.VMEM((slots, 2, rows, LANES), jnp.int32),
                 pltpu.SemaphoreType.REGULAR((2,)),
                 pltpu.SemaphoreType.DMA,
                 pltpu.SemaphoreType.DMA((LEVELS + 1,)),

time: 9.58 us -> 9.51 us (level)
  no operation moved by 1% of the time
where the time goes in v1:
time: 9.51 us; the launch traced here: 9.33 us
  Pallas kernels  8.72 us (92%)
  local copies, waits for them, and re-layouts  0.6 us (6%)
    pallas_call x1, Pallas kernels, on_device(): pl.pallas_call(functools.partial(kernel, n, slots, share, across), out_sh...  8.72 us
    unnamed x1, local copies, waits for them, and re-layouts  0.6 us

profile of v1, /device:TPU:0, one launch (start us, length us, event | category | flops | bytes accessed | tf_op | source)
XLA Modules:
  0.0 9.3 jit_solution(159681754248527577)
XLA Ops:
  0.0 8.7 %shard_map.55 = f32[1,2,1024]{2,1,0:T(2,128)S(1)} custom-call(s32[16]{0:T(128)} %assign_hbm.1, s32[16,2048]{1,0:T(8,128)} %database_hbm.1, s32[8,16]{1,0:T(8,128)} %queries_hbm.1, s32[8,512]{1,0:T(8,128)} %keys_hbm.1, s32[2,1024]{1,0:T(2,128)} %hint_hbm.1), custom_call_target="tpu_custom_call" | custom-call | tf_op jit(solution)/shard_map/pallas_call | solution.py:425
  8.7 0.6 %copy.7 = f32[1,2,1024]{2,1,0:T(2,128)} copy(f32[1,2,1024]{2,1,0:T(2,128)S(1)} %shard_map.55) | data formatting | bytes 16384

commit v2 on v1

--- a/solution.py
+++ b/solution.py
@@ -145,9 +145,27 @@
     return out
 
 
+def fold_tiles(tiles):
+    line = iota(tiles[0].shape, 0)
+    apart = len(tiles) // 2
+    while apart:
+        low = jnp.bitwise_and(line, apart) == 0
+        folded = []
+        for first, second in zip(tiles[:apart], tiles[apart:]):
+            kept = jnp.where(low, first, second)
+            other = jnp.where(low, second, first)
+            down = pltpu.roll(other, apart, 0)
+            if 2 * apart < line.shape[0]:
+                down = jnp.where(low, pltpu.roll(other, line.shape[0] - apart, 0), down)
+            folded.append(kept + down)
+        tiles = folded
+        apart //= 2
+    return tiles[0]
+
+
 def kernel(
     n, slots, share, width, assign_hbm, database_hbm, queries_hbm, keys_hbm, hint_hbm, out,
-    assign, database, queries, keys, hint, loaded, unit_part, unit_keys, masks,
+    assign, query_scalars, database, queries, keys, hint, loaded, unit_part, unit_keys, masks,
     ans_send, key_send, ans_recv, key_recv, key_words, toeplitz, tail, held,
     ready, ans_got, key_got,
 ):
@@ -159,8 +177,8 @@
     key_pitch = unit_keys.shape[1]
     unit_key_rows = unit_keys.reshape(clients * polys * key_pitch, LANES)
     unit_part_rows = unit_part.reshape(clients * polys * rows, LANES)
-    chunks = 4
-    chunk = database.shape[1] // chunks
+    pieces = max(1, 4 // polys)
+    piece = cycle // pieces
     size = 2
     planes = n // size
     few = n <= LANES // 8
@@ -176,24 +194,27 @@
     def each(count, body, start=0):
         lax.fori_loop(start, count, lambda i, c: (body(i), c)[1], 0, unroll=few)
     loads = [
-        pltpu.make_async_copy(source, target, loaded.at[min(i // 2, 1)])
+        pltpu.make_async_copy(source, target, loaded.at[i // 3])
         for i, (source, target) in enumerate(
             (
                 (assign_hbm, assign),
+                (queries_hbm, query_scalars),
                 (keys_hbm, keys),
-                (database_hbm, database),
                 (queries_hbm, queries),
                 (hint_hbm, hint),
             )
         )
     ]
-    for i, load in enumerate(loads):
-        if i == 2:
-            for j in range(chunks):
-                at = pl.ds(j * chunk, chunk)
-                pltpu.make_async_copy(database_hbm.at[:, at], database.at[:, at], loaded.at[1]).start()
-        else:
-            load.start()
+    for load in loads[:3]:
+        load.start()
+    for p in range(polys):
+        for j in range(pieces):
+            at = pl.ds(j * piece, piece)
+            pltpu.make_async_copy(
+                database_hbm.at[:, pl.ds(p * cycle + j * piece, piece)], database.at[p, :, at], loaded.at[1]
+            ).start()
+    for load in loads[3:]:
+        load.start()
     def span(start, stop, body):
         lax.fori_loop(start, stop, lambda i, c: (body(i), c)[1], 0)
 
@@ -232,8 +253,8 @@
 
     announce(0, planes // 2)
     announce(1, planes)
-    loads[0].wait()
-    loads[1].wait()
+    for load in loads[:3]:
+        load.wait()
     lane_owner = iota((clients, LANES), 1) // (LANES // share)
     for j in range(key_rows):
         tile = keys[:, j * LANES : (j + 1) * LANES]
@@ -249,7 +270,6 @@
     def stage_answers(owner):
         for k in range(slots):
             ans_send[owner, k * rows : (k + 1) * rows, :] = unit_part[assign[owner * slots + k]]
-    each(n, stage_keys)
 
     def send_keys(there):
         pltpu.make_async_remote_copy(
@@ -291,27 +311,52 @@
             if stage:
                 start = jnp.maximum(start, jnp.where(along < height // 2, height // 2, 0))
             on_chips(start, height // 2 if stage == 0 else height, column, send)
+    for core in range(size):
+        stage_keys(core)
     to_first(send_keys)
+    each(n, stage_keys, size)
     pltpu.make_async_copy(key_send.at[me], key_recv.at[me], key_got.at[kind_held]).start()
-    for load in loads[2:]:
+
+    line = iota((columns, LANES), 0)
+    first_units = [assign[core * slots + k] for core in range(size) for k in range(slots)]
+    first_queries = []
+    for unit in first_units:
+        client = lax.div(unit, polys)
+        column = jnp.zeros((columns, LANES), jnp.int32)
+        for j in range(columns):
+            column = jnp.where(line == j, query_scalars[client, j], column)
+        first_queries.append(column)
+    pltpu.make_async_copy(database, database, loaded.at[1]).wait()
+    for load in loads[3:]:
         load.wait()
+    for i, (unit, column) in enumerate(zip(first_units, first_queries)):
+        bytes_held = database[lax.rem(unit, polys)]
+        tiles = []
+        for q in range(rows):
+            terms = bytes_held[:, q * LANES : (q + 1) * LANES] * column
+            tile = terms[:rows]
+            for j in range(rows, columns, rows):
+                tile = tile + terms[j : j + rows]
+            tiles.append(tile)
+        core, k = divmod(i, slots)
+        ans_send[core, k * rows : (k + 1) * rows, :] = fold_tiles(tiles)
+    to_first(send_answers)
     query_words = queries[...]
     query_bytes = jnp.concatenate(
         [byte_of(query_words, b) for b in range(WORD_BYTES)], axis=0
     ).astype(jnp.bfloat16)
-    products = jnp.dot(
-        query_bytes,
-        database[...].astype(jnp.float32).astype(jnp.bfloat16),
-        preferred_element_type=jnp.float32,
-    ).astype(jnp.int32)
-    partial = products[:clients]
-    for b in range(1, WORD_BYTES):
-        partial = partial + jnp.left_shift(products[b * clients : (b + 1) * clients], 8 * b)
-    for j in range(polys * rows):
-        unit_part_rows[pl.ds(j, clients, stride=polys * rows), :] = partial[:, j * LANES : (j + 1) * LANES]
-    for core in range(size):
-        stage_answers(core)
-    to_first(send_answers)
+    for p in range(polys):
+        products = jnp.dot(
+            query_bytes,
+            database[p].astype(jnp.float32).astype(jnp.bfloat16),
+            preferred_element_type=jnp.float32,
+        ).astype(jnp.int32)
+        partial = products[:clients]
+        for b in range(1, WORD_BYTES):
+            partial = partial + jnp.left_shift(products[b * clients : (b + 1) * clients], 8 * b)
+        for q in range(rows):
+            rows_at = pl.ds(p * rows + q, clients, stride=polys * rows)
+            unit_part_rows[rows_at, :] = partial[:, q * LANES : (q + 1) * LANES]
     each(n, stage_answers, size)
     to_early(send_keys)
     to_early(send_answers)
@@ -429,7 +474,8 @@
             out_specs=pl.BlockSpec(memory_space=pltpu.VMEM),
             scratch_shapes=[
                 pltpu.SMEM(assignment.shape, jnp.int32),
-                pltpu.VMEM(database.shape, jnp.int32),
+                pltpu.SMEM(queries.shape, jnp.int32),
+                pltpu.VMEM((polys, database.shape[0], cycle), jnp.int32),
                 pltpu.VMEM(queries.shape, jnp.int32),
                 pltpu.VMEM(key_rows.shape, jnp.int32),
                 pltpu.VMEM(hint.shape, jnp.int32),

time: 9.51 us -> 9.47 us (level)
  no operation moved by 1% of the time
where the time goes in v2:
time: 9.47 us; the launch traced here: 9.29 us
  Pallas kernels  8.68 us (92%)
  local copies, waits for them, and re-layouts  0.6 us (6%)
    pallas_call x1, Pallas kernels, on_device(): pl.pallas_call(functools.partial(kernel, n, slots, share, across), out_sh...  8.68 us
    unnamed x1, local copies, waits for them, and re-layouts  0.6 us

profile of v2, /device:TPU:0, one launch (start us, length us, event | category | flops | bytes accessed | tf_op | source)
XLA Modules:
  0.0 9.3 jit_solution(9123507470262571625)
XLA Ops:
  0.0 8.7 %shard_map.55 = f32[1,2,1024]{2,1,0:T(2,128)S(1)} custom-call(s32[16]{0:T(128)} %assign_hbm.1, s32[16,2048]{1,0:T(8,128)} %database_hbm.1, s32[8,16]{1,0:T(8,128)} %queries_hbm.1, s32[8,512]{1,0:T(8,128)} %keys_hbm.1, s32[2,1024]{1,0:T(2,128)} %hint_hbm.1), custom_call_target="tpu_custom_call" | custom-call | tf_op jit(solution)/shard_map/pallas_call | solution.py:470
  8.7 0.6 %copy.7 = f32[1,2,1024]{2,1,0:T(2,128)} copy(f32[1,2,1024]{2,1,0:T(2,128)S(1)} %shard_map.55) | data formatting | bytes 16384

commit v3 on v2

--- a/solution.py
+++ b/solution.py
@@ -13,6 +13,7 @@
 WORD_BYTES = 4
 DIGIT_BYTES = WORD_BYTES // DIGITS
 SPAN = LANES // DIGIT_BYTES
+MXUS = 2
 
 
 def iota(shape, axis):
@@ -98,19 +99,38 @@
     return jnp.concatenate(blocks, axis=0).astype(jnp.bfloat16)
 
 
-def switch(toeplitz, key_polys, rows):
-    sides = len(key_polys[0])
-    products = jnp.dot(
-        key_side(key_polys), toeplitz, preferred_element_type=jnp.float32
-    ).astype(jnp.int32)
+def staged_product(table, count, make_side):
+    width = DIGIT_BYTES * LANES
+    tiles = table.shape[1] // width
+
+    def body(*sums):
+        for i in range(tiles):
+            pltpu.matmul_push_rhs(
+                table[:, i * width : (i + 1) * width], staging_register=i // MXUS, mxu_index=i % MXUS
+            )
+        side = make_side()
+        for i in range(tiles):
+            pltpu.matmul_acc_lhs(sums[i], side, load_staged_rhs=i // MXUS)
+        parts = [pltpu.matmul_pop(one) for one in sums]
+        return jnp.concatenate(parts, axis=1).astype(jnp.int32)
+
+    return pl.run_scoped(
+        body, *(pltpu.ACC(i % MXUS)((count, width), jnp.float32) for i in range(tiles))
+    )
+
+
+def switch(toeplitz, make_keys, rows):
+    products = staged_product(
+        toeplitz, WORD_BYTES * 2 * DIGIT_BYTES * rows, lambda: key_side(make_keys())
+    )
     lane = iota((rows, LANES), 1)
     sums = []
-    for p in range(sides):
+    for p in range(2):
         total = jnp.zeros((rows, LANES), jnp.int32)
         for h in range(DIGIT_BYTES):
             words = None
             for s in range(WORD_BYTES):
-                at = ((s * sides + p) * DIGIT_BYTES + h) * rows
+                at = ((s * 2 + p) * DIGIT_BYTES + h) * rows
                 term = jnp.left_shift(products[at : at + rows], 8 * s)
                 words = term if words is None else words + term
             out = words[:, :LANES]
@@ -125,17 +145,19 @@
     return sums
 
 
-def switch_tail(table, words):
-    rows = words.shape[0]
-    moved = [jnp.left_shift(words, 8 * a) for a in range(DIGIT_BYTES)]
-    side = jnp.concatenate(
-        [
-            jnp.concatenate([byte_of(part, s) for part in moved], axis=1)
-            for s in range(WORD_BYTES)
-        ],
-        axis=0,
-    ).astype(jnp.bfloat16)
-    products = jnp.dot(side, table, preferred_element_type=jnp.float32).astype(jnp.int32)
+def switch_tail(table, make_words, rows):
+    def side():
+        words = make_words()
+        moved = [jnp.left_shift(words, 8 * a) for a in range(DIGIT_BYTES)]
+        return jnp.concatenate(
+            [
+                jnp.concatenate([byte_of(part, s) for part in moved], axis=1)
+                for s in range(WORD_BYTES)
+            ],
+            axis=0,
+        ).astype(jnp.bfloat16)
+
+    products = staged_product(table, WORD_BYTES * rows, side)
     total = products[:rows]
     for s in range(1, WORD_BYTES):
         total = total + jnp.left_shift(products[s * rows : (s + 1) * rows], 8 * s)
@@ -165,18 +187,17 @@
 
 def kernel(
     n, slots, share, width, assign_hbm, database_hbm, queries_hbm, keys_hbm, hint_hbm, out,
-    assign, query_scalars, database, queries, keys, hint, loaded, unit_part, unit_keys, masks,
+    assign, query_scalars, database, keys, hint, loaded, unit_part, unit_keys, masks,
     ans_send, key_send, ans_recv, key_recv, key_words, toeplitz, tail, held,
     ready, ans_got, key_got,
 ):
     me = lax.axis_index("col")
-    clients, columns = queries.shape
+    clients, columns = query_scalars.shape
     polys, cycle = hint.shape
     rows = cycle // LANES
     key_rows = key_send.shape[1] // slots
     key_pitch = unit_keys.shape[1]
     unit_key_rows = unit_keys.reshape(clients * polys * key_pitch, LANES)
-    unit_part_rows = unit_part.reshape(clients * polys * rows, LANES)
     pieces = max(1, 4 // polys)
     piece = cycle // pieces
     size = 2
@@ -200,7 +221,6 @@
                 (assign_hbm, assign),
                 (queries_hbm, query_scalars),
                 (keys_hbm, keys),
-                (queries_hbm, queries),
                 (hint_hbm, hint),
             )
         )
@@ -318,19 +338,15 @@
     pltpu.make_async_copy(key_send.at[me], key_recv.at[me], key_got.at[kind_held]).start()
 
     line = iota((columns, LANES), 0)
-    first_units = [assign[core * slots + k] for core in range(size) for k in range(slots)]
-    first_queries = []
-    for unit in first_units:
-        client = lax.div(unit, polys)
+
+    def query_column(client):
         column = jnp.zeros((columns, LANES), jnp.int32)
         for j in range(columns):
             column = jnp.where(line == j, query_scalars[client, j], column)
-        first_queries.append(column)
-    pltpu.make_async_copy(database, database, loaded.at[1]).wait()
-    for load in loads[3:]:
-        load.wait()
-    for i, (unit, column) in enumerate(zip(first_units, first_queries)):
-        bytes_held = database[lax.rem(unit, polys)]
+        return column
+
+    def answer(poly, column):
+        bytes_held = database[poly]
         tiles = []
         for q in range(rows):
             terms = bytes_held[:, q * LANES : (q + 1) * LANES] * column
@@ -338,27 +354,28 @@
             for j in range(rows, columns, rows):
                 tile = tile + terms[j : j + rows]
             tiles.append(tile)
+        return fold_tiles(tiles)
+
+    first_units = [assign[core * slots + k] for core in range(size) for k in range(slots)]
+    first_queries = [query_column(lax.div(unit, polys)) for unit in first_units]
+    pltpu.make_async_copy(database, database, loaded.at[1]).wait()
+    loads[3].wait()
+    for i, (unit, column) in enumerate(zip(first_units, first_queries)):
         core, k = divmod(i, slots)
-        ans_send[core, k * rows : (k + 1) * rows, :] = fold_tiles(tiles)
+        ans_send[core, k * rows : (k + 1) * rows, :] = answer(lax.rem(unit, polys), column)
     to_first(send_answers)
-    query_words = queries[...]
-    query_bytes = jnp.concatenate(
-        [byte_of(query_words, b) for b in range(WORD_BYTES)], axis=0
-    ).astype(jnp.bfloat16)
-    for p in range(polys):
-        products = jnp.dot(
-            query_bytes,
-            database[p].astype(jnp.float32).astype(jnp.bfloat16),
-            preferred_element_type=jnp.float32,
-        ).astype(jnp.int32)
-        partial = products[:clients]
-        for b in range(1, WORD_BYTES):
-            partial = partial + jnp.left_shift(products[b * clients : (b + 1) * clients], 8 * b)
-        for q in range(rows):
-            rows_at = pl.ds(p * rows + q, clients, stride=polys * rows)
-            unit_part_rows[rows_at, :] = partial[:, q * LANES : (q + 1) * LANES]
+    to_early(send_keys)
+
+    def client_answers(client):
+        column = query_column(client)
+
+        def poly_answer(poly):
+            unit_part[client * polys + poly] = answer(poly, column)
+
+        each(polys, poly_answer)
+
+    each(clients, client_answers)
     each(n, stage_answers, size)
-    to_early(send_keys)
     to_early(send_answers)
     pltpu.make_async_copy(ans_send.at[me], ans_recv.at[me], ans_got).start()
     for p in range(polys):
@@ -408,8 +425,12 @@
             fill_toeplitz(automorph(mask, 0), toeplitz)
         added = []
         for level in range(last):
-            gather_keys(k, level, level * level_blocks, (level + 1) * level_blocks)
-            to_mask, to_value = switch(toeplitz[...], key_polys(level), rows)
+
+            def make_keys():
+                gather_keys(k, level, level * level_blocks, (level + 1) * level_blocks)
+                return key_polys(level)
+
+            to_mask, to_value = switch(toeplitz, make_keys, rows)
             mask = mask + to_mask
             added.append(to_value)
             turned = automorph(mask, level + 1)
@@ -417,22 +438,32 @@
         early, late = n - level_blocks, n - poly_blocks
         @pl.when(chip > 0)
         def _():
-            gather_keys(k, last, early, late)
-            gather_keys(k, LEVELS, late, n)
-            to_mask, to_value = switch(toeplitz[...], key_polys(last), rows)
+            def make_keys():
+                gather_keys(k, last, early, late)
+                gather_keys(k, LEVELS, late, n)
+                return key_polys(last)
+
+            to_mask, to_value = switch(toeplitz, make_keys, rows)
             held[k, 0] = mask + to_mask
             held[k, 1] = to_value
 
         @pl.when(chip == 0)
         def _():
-            gather_keys(k, last, early, late)
-            polys_held = key_polys(last)
-            polys_held[-1][-1] = [jnp.zeros((rows, LANES), jnp.int32)] * DIGIT_BYTES
-            to_mask, to_value = switch(toeplitz[...], polys_held, rows)
+            def make_keys():
+                gather_keys(k, last, early, late)
+                polys_held = key_polys(last)
+                polys_held[-1][-1] = [jnp.zeros((rows, LANES), jnp.int32)] * DIGIT_BYTES
+                return polys_held
+
+            to_mask, to_value = switch(toeplitz, make_keys, rows)
             held[k, 0] = mask + to_mask
             fill_tail(turned, tail)
-            gather_keys(k, LEVELS, late, n)
-            held[k, 1] = to_value + switch_tail(tail[...], key_poly(last, DIGITS - 1, 1))
+
+            def tail_words():
+                gather_keys(k, LEVELS, late, n)
+                return key_poly(last, DIGITS - 1, 1)
+
+            held[k, 1] = to_value + switch_tail(tail, tail_words, rows)
 
         switched.append(added)
     wait_blocks(ans_recv, ans_got, 0, n)
@@ -476,7 +507,6 @@
                 pltpu.SMEM(assignment.shape, jnp.int32),
                 pltpu.SMEM(queries.shape, jnp.int32),
                 pltpu.VMEM((polys, database.shape[0], cycle), jnp.int32),
-                pltpu.VMEM(queries.shape, jnp.int32),
                 pltpu.VMEM(key_rows.shape, jnp.int32),
                 pltpu.VMEM(hint.shape, jnp.int32),
                 pltpu.SemaphoreType.DMA((2,)),

time: 9.47 us -> 9.4 us (level)
  no operation moved by 1% of the time
where the time goes in v3:
time: 9.4 us; the launch traced here: 9.22 us
  Pallas kernels  8.61 us (92%)
  local copies, waits for them, and re-layouts  0.6 us (6%)
    pallas_call x1, Pallas kernels, on_device(): pl.pallas_call(functools.partial(kernel, n, slots, share, across), out_sh...  8.61 us
    unnamed x1, local copies, waits for them, and re-layouts  0.6 us

profile of v3, /device:TPU:0, one launch (start us, length us, event | category | flops | bytes accessed | tf_op | source)
XLA Modules:
  0.0 9.2 jit_solution(10474379827338459899)
XLA Ops:
  0.0 8.6 %shard_map.55 = f32[1,2,1024]{2,1,0:T(2,128)S(1)} custom-call(s32[16]{0:T(128)} %assign_hbm.1, s32[16,2048]{1,0:T(8,128)} %database_hbm.1, s32[8,16]{1,0:T(8,128)} %queries_hbm.1, s32[8,512]{1,0:T(8,128)} %keys_hbm.1, s32[2,1024]{1,0:T(2,128)} %hint_hbm.1), custom_call_target="tpu_custom_call" | custom-call | tf_op jit(solution)/shard_map/pallas_call | solution.py:501
  8.6 0.6 %copy.7 = f32[1,2,1024]{2,1,0:T(2,128)} copy(f32[1,2,1024]{2,1,0:T(2,128)S(1)} %shard_map.55) | data formatting | bytes 16384

commit v4 on v3

--- a/solution.py
+++ b/solution.py
@@ -185,11 +185,15 @@
     return tiles[0]
 
 
-def kernel(
+def kernel(*refs):
+    pl.run_scoped(functools.partial(scoped, *refs), pltpu.SemaphoreType.DMA((2,)))
+
+
+def scoped(
     n, slots, share, width, assign_hbm, database_hbm, queries_hbm, keys_hbm, hint_hbm, out,
-    assign, query_scalars, database, keys, hint, loaded, unit_part, unit_keys, masks,
+    assign, query_scalars, database, keys, hint, unit_part, unit_keys, masks,
     ans_send, key_send, ans_recv, key_recv, key_words, toeplitz, tail, held,
-    ready, ans_got, key_got,
+    ready, ans_got, key_got, loaded,
 ):
     me = lax.axis_index("col")
     clients, columns = query_scalars.shape
@@ -331,10 +335,8 @@
             if stage:
                 start = jnp.maximum(start, jnp.where(along < height // 2, height // 2, 0))
             on_chips(start, height // 2 if stage == 0 else height, column, send)
-    for core in range(size):
-        stage_keys(core)
+    each(n, stage_keys)
     to_first(send_keys)
-    each(n, stage_keys, size)
     pltpu.make_async_copy(key_send.at[me], key_recv.at[me], key_got.at[kind_held]).start()
 
     line = iota((columns, LANES), 0)
@@ -466,19 +468,23 @@
             held[k, 1] = to_value + switch_tail(tail, tail_words, rows)
 
         switched.append(added)
+
+    def write(k, index, words):
+        scaled = words.astype(jnp.float32) * 2.0 ** (-32)
+        for q in range(rows):
+            out[k, index : index + 1, q * LANES : (q + 1) * LANES] = scaled[q : q + 1]
+
+    for k in range(slots):
+        write(k, 0, held[k, 0])
     wait_blocks(ans_recv, ans_got, 0, n)
     for k, added in enumerate(switched):
-        mask = held[k, 0]
         added = added + [held[k, 1]]
         value = ans_recv[0, k * rows : (k + 1) * rows, :]
         for j in range(1, n):
             value = value + ans_recv[j, k * rows : (k + 1) * rows, :]
         for level in range(LEVELS):
             value = value + automorph(value, level) + added[level]
-        for index, words in enumerate((mask, value)):
-            scaled = words.astype(jnp.float32) * 2.0 ** (-32)
-            for q in range(rows):
-                out[k, index : index + 1, q * LANES : (q + 1) * LANES] = scaled[q : q + 1]
+        write(k, 1, value)
     wait_blocks(key_send, sent, 0, n - 1)
     wait_blocks(ans_send, sent, 0, n - 1)
 
@@ -509,7 +515,6 @@
                 pltpu.VMEM((polys, database.shape[0], cycle), jnp.int32),
                 pltpu.VMEM(key_rows.shape, jnp.int32),
                 pltpu.VMEM(hint.shape, jnp.int32),
-                pltpu.SemaphoreType.DMA((2,)),
                 pltpu.VMEM((polys * clients, rows, LANES), jnp.int32),
                 pltpu.VMEM((polys * clients, -(-tiles // 8) * 8, LANES), jnp.int32),
                 pltpu.VMEM((polys, rows, LANES), jnp.int32),

time: 9.4 us -> 9.41 us (level)
  no operation moved by 1% of the time
where the time goes in v4:
time: 9.41 us; the launch traced here: 9.23 us
  Pallas kernels  8.62 us (92%)
  local copies, waits for them, and re-layouts  0.6 us (6%)
    pallas_call x1, Pallas kernels, on_device(): pl.pallas_call(functools.partial(kernel, n, slots, share, across), out_sh...  8.62 us
    unnamed x1, local copies, waits for them, and re-layouts  0.6 us

profile of v4, /device:TPU:0, one launch (start us, length us, event | category | flops | bytes accessed | tf_op | source)
XLA Modules:
  0.0 9.2 jit_solution(7587796681725803463)
XLA Ops:
  0.0 8.6 %shard_map.55 = f32[1,2,1024]{2,1,0:T(2,128)S(1)} custom-call(s32[16]{0:T(128)} %refs_0_.1, s32[16,2048]{1,0:T(8,128)} %refs_1_.1, s32[8,16]{1,0:T(8,128)} %refs_2_.1, s32[8,512]{1,0:T(8,128)} %refs_3_.1, s32[2,1024]{1,0:T(2,128)} %refs_4_.1), custom_call_target="tpu_custom_call" | custom-call | tf_op jit(solution)/shard_map/pallas_call | solution.py:507
  8.6 0.6 %copy.7 = f32[1,2,1024]{2,1,0:T(2,128)} copy(f32[1,2,1024]{2,1,0:T(2,128)S(1)} %shard_map.55) | data formatting | bytes 16384
